TPU v7x, 256 devices: a whole 4x4x8 slice. The times are simulated.
256 devices in a mesh: loop: 32 (over z, x_lo, core), group: 8 (over y, x_hi).
Axes of the slice: x: 4 (x_hi: 2, x_lo: 2; x = x_hi * 2 + x_lo), y: 4, z: 8, core: 2. Of those that a mesh axis runs over, the one named last changes fastest.
Arguments:
- images: bfloat16 [8, 256, 7, 7, 1536], P('group', 'loop'), as said below
- targets: int32 [8, 256], P('group'), may hold values from 0 to 131071, as said below
- kernel: bfloat16 [7, 7, 1536], replicated, may hold values from -0.875 to 0.875
- projection: bfloat16 [1536, 768], replicated, as said below
- captions: bfloat16 [131072, 768], P('loop'), as said below
Outputs:
- loss: float32 [8, 256], P('group', 'loop')
- image_grad: bfloat16 [8, 256, 7, 7, 1536], P('group', 'loop')
- kernel_grad: float32 [1536, 49], P(('loop', 'group'))
Inputs may be any that keep to these rules, and one draw needn't show every extreme that they name: targets index captions of the whole gallery. `images`: finite real values. `projection`: finite real values. `captions`: finite real values, no caption all zero.
All inputs are finite; a program needn't handle non-finite values.
Results may differ from a plain program's by a relative error of at most 0.0066.
Values may be sent and summed in bfloat16 or wider, within the bound.
A program may use at most 64 MiB of HBM per device.

v0:
```python
import jax
import jax.numpy as jnp
from jax import lax
from jax.sharding import PartitionSpec as P

logit_sharpness = 20.0


def depthwise(padded, kernel):
    reach = kernel.shape[0]
    side = padded.shape[1] - reach + 1
    total = jnp.zeros((padded.shape[0], side, side, padded.shape[3]), jnp.float32)
    for row_off in range(reach):
        for col_off in range(reach):
            window = padded[:, row_off : row_off + side, col_off : col_off + side, :].astype(
                jnp.float32
            )
            total = total + window * kernel[row_off, col_off].astype(jnp.float32)
    return total


def forward(pixels, kernel, projection):
    margin = kernel.shape[0] // 2
    padded = jnp.pad(pixels, ((0, 0), (margin, margin), (margin, margin), (0, 0)))
    hidden = depthwise(padded, kernel)
    centre = hidden - jnp.mean(hidden, -1, keepdims=True)
    scale_inv = lax.rsqrt(jnp.mean(centre * centre, -1, keepdims=True) + 1e-06)
    normed = centre * scale_inv
    pooled = jnp.mean(pixels.astype(jnp.float32) + normed, axis=(1, 2)).astype(jnp.bfloat16)
    embedded = jnp.dot(pooled, projection, preferred_element_type=jnp.float32)
    inv_norm = lax.rsqrt(jnp.sum(embedded * embedded, -1, keepdims=True) + 1e-06)
    return (padded, normed, scale_inv, embedded, inv_norm)


def backward(padded, normed, scale_inv, embedded, inv_norm, kernel, projection, query_gradient):
    unit = embedded * inv_norm
    emb_grad = (
        (query_gradient - unit * jnp.sum(unit * query_gradient, -1, keepdims=True)) * inv_norm
    ).astype(jnp.bfloat16)
    pooled_grad = lax.dot_general(
        emb_grad, projection, (((1,), (1,)), ((), ())), preferred_element_type=jnp.float32
    )
    side = normed.shape[1]
    out_grad = (pooled_grad / (side * side))[:, None, None, :]
    hidden_grad = scale_inv * (
        out_grad
        - jnp.mean(out_grad, -1, keepdims=True)
        - normed * jnp.mean(normed * out_grad, -1, keepdims=True)
    )
    reach = kernel.shape[0]
    margin = reach // 2
    grad_pad = jnp.pad(hidden_grad, ((0, 0), (margin, margin), (margin, margin), (0, 0)))
    input_grad = out_grad + depthwise(grad_pad, kernel[::-1, ::-1])
    taps = []
    for row_off in range(reach):
        for col_off in range(reach):
            window = padded[:, row_off : row_off + side, col_off : col_off + side, :].astype(
                jnp.float32
            )
            taps.append(jnp.sum(window * hidden_grad, axis=(0, 1, 2)))
    return (input_grad, jnp.stack(taps, 0).T)


def normalize(captions):
    values = captions.astype(jnp.float32)
    return (values * lax.rsqrt(jnp.sum(values * values, -1, keepdims=True) + 1e-06)).astype(
        jnp.bfloat16
    )


def shards(images, targets, kernel, projection, captions):
    pixels = images[0]
    group_targets = targets[0]
    own_rows = pixels.shape[0]
    cap_rows = captions.shape[0]
    group_rows = group_targets.shape[0]
    padded, normed, scale_inv, embedded, inv_norm = forward(pixels, kernel, projection)
    query = (embedded * inv_norm).astype(jnp.bfloat16)
    normalized_caption_vectors = normalize(captions)
    similarity_scores = logit_sharpness * lax.dot_general(
        lax.all_gather(query, "loop", axis=0, tiled=True),
        normalized_caption_vectors,
        (((1,), (1,)), ((), ())),
        preferred_element_type=jnp.float32,
    )
    col_part = jnp.sum(jnp.exp(similarity_scores), 0)
    col_log = jnp.log(lax.psum(col_part, "group"))
    weight = jnp.exp(similarity_scores - col_log)
    local_index = group_targets - lax.axis_index("loop") * cap_rows
    onehot = (
        local_index[:, None] == lax.broadcasted_iota(jnp.int32, (group_rows, cap_rows), 1)
    ).astype(jnp.float32)
    row_part = jnp.sum(weight, 1)
    target_part = jnp.sum(onehot * (similarity_scores - col_log), 1)
    row_sum, target_logit = lax.psum((row_part, target_part), "loop")
    loss_group = jnp.log(row_sum) - target_logit
    own_start = lax.axis_index("loop") * own_rows
    own_loss = lax.dynamic_slice_in_dim(loss_group, own_start, own_rows, 0)
    grad = weight / row_sum[:, None] - onehot
    col_grad = lax.psum(jnp.sum(grad, 0), "group")
    similarity_gradient = (grad - weight * col_grad).astype(jnp.bfloat16)
    incomplete_gradient = logit_sharpness * jnp.dot(
        similarity_gradient, normalized_caption_vectors, preferred_element_type=jnp.float32
    )
    summed = lax.psum(incomplete_gradient, "loop")
    query_gradient = lax.dynamic_slice_in_dim(summed, own_start, own_rows, 0)
    input_grad, kernel_terms = backward(
        padded, normed, scale_inv, embedded, inv_norm, kernel, projection, query_gradient
    )
    kernel_share = lax.psum_scatter(
        kernel_terms, ("loop", "group"), scatter_dimension=0, tiled=True
    )
    return (own_loss[None], input_grad.astype(jnp.bfloat16)[None], kernel_share)


def solution(mesh):
    placed = (P("group", "loop", None, None, None), P("group", None), P(), P(), P("loop", None))
    return jax.shard_map(
        shards,
        mesh=mesh,
        in_specs=placed,
        out_specs=(
            P("group", "loop"),
            P("group", "loop", None, None, None),
            P(("loop", "group"), None),
        ),
        check_vma=False,
    )
```

profile of v0, /device:TPU:1, one launch (start us, length us, event | category | flops | bytes accessed | tf_op | source)
XLA Modules:
  0.0 739.3 jit_solution(11930092785954452918)
XLA Ops:
  7.2 0.0 copy-start
  7.2 0.0 all-reduce.6.cloned.1.call-start
  7.2 1.2 convert_reduce_fusion.46
  8.5 1.5 convert_reduce_fusion.48
  10.0 1.6 convert_reduce_fusion.47
  11.6 0.0 copy-start.3
  11.6 31.9 %fusion.216 = (f32[8,7,7]{0,2,1:T(8,128)S(1)}, f32[8,7,7,1536]{3,0,2,1:T(8,128)S(1)}) fusion(f32[1536]{0:T(1024)S(1)} %get-tuple-element.107, f32[1536]{0:T(1024)S(1)} %get-tuple-element.108, f32[1536]{0:T(1024)S(1)} %get-tuple-element.61, f32[1536]{0:T(1024)S(1)} %get-tuple-element.62, f32[1536]{0:T(1024)S(1)} %get-tuple-element.63, ...), kind=kLoop, calls=%fused_computation.486 | loop fusion | flops 88510072 | bytes 3915296 | tf_op jit(solution)/shard_map/reduce_sum | solution.py:26
  43.5 0.0 copy-start.1
  43.5 0.4 multiply_reduce_fusion.1
  43.9 0.0 copy-done.3
  43.9 0.0 copy-start.6
  43.9 0.5 fusion.103
  44.4 0.5 copy-done.1
  44.9 0.0 copy-done
  44.9 0.5 multiply_reduce_fusion.3
  45.5 0.1 multiply_convert_fusion.3
  45.6 39.6 %all_gather.3 = bf16[256,768]{1,0:T(8,128)(2,1)S(1)} all-gather(bf16[8,768]{1,0:T(8,128)(2,1)S(1)} %multiply_convert_fusion.3), channel_id=1, replica_groups=mesh['loop'=32,'group'=8] {'loop'}, dimensions={0}, use_global_device_ids=true | all-gather | bytes 405504 | tf_op jit(solution)/shard_map/all_gather | solution.py:81
  85.2 0.0 copy-done.6
  85.2 1.3 fusion
  86.5 3.8 exponential_reduce_fusion
  90.4 34.7 %psum.35 = f32[4096]{0:T(1024)S(1)} all-reduce(f32[4096]{0:T(1024)S(1)} %get-tuple-element.114), channel_id=1, replica_groups=mesh['loop'=32,'group'=8] {'group'}, use_global_device_ids=true, to_apply=%region_6.7 | all-reduce | flops 4096 | bytes 32768 | tf_op jit(solution)/shard_map/psum | solution.py:87
  125.1 2.8 fusion.3
  127.9 59.8 %psum.36 = f32[256]{0:T(256)S(1)} all-reduce(f32[256]{0:T(256)S(1)} %fusion.3), channel_id=1, replica_groups=mesh['loop'=32,'group'=8] {'loop'}, use_global_device_ids=true, to_apply=%region_8.9 | all-reduce | flops 256 | bytes 2048 | tf_op jit(solution)/shard_map/psum | solution.py:95
  187.7 0.0 copy-done.7
  187.7 4.2 fusion.2
  191.9 30.1 %psum.38 = f32[4096]{0:T(1024)S(1)} all-reduce(f32[4096]{0:T(1024)S(1)} %get-tuple-element.9), channel_id=1, replica_groups=mesh['loop'=32,'group'=8] {'group'}, use_global_device_ids=true, to_apply=%region_12.13 | all-reduce | flops 4096 | bytes 32768 | tf_op jit(solution)/shard_map/psum | solution.py:100
  222.0 8.0 %fusion.206 = f32[256,768]{1,0:T(8,128)} fusion(bf16[4096,768]{1,0:T(8,128)(2,1)} %param.9, f32[4096]{0:T(1024)S(1)} %add_rsqrt_fusion.1, f32[256,4096]{1,0:T(8,128)} %get-tuple-element.115, f32[4096]{0:T(1024)S(1)} %psum.38, f32[256]{0:T(256)S(1)} %psum.36, s32[256]{0:T(256)S(1)} %bitcast.20, f32[4096]{0:T(1024)S(1)} %log.6), kind=kOutput, calls=%fused_computation.413 | convolution fusion | flops 1628635136 | bytes 11323392 | tf_op jit(solution)/shard_map/dot_general | solution.py:102
  230.0 0.0 all-reduce.6.cloned.1.call-update
  230.0 0.0 all-reduce.8.cloned.1.call-start
  230.1 59.9 %psum.37 = f32[256]{0:T(256)S(1)} all-reduce(f32[256]{0:T(256)S(1)} %get-tuple-element.10), channel_id=1, replica_groups=mesh['loop'=32,'group'=8] {'loop'}, use_global_device_ids=true, to_apply=%region_10.11 | all-reduce | flops 256 | bytes 2048 | tf_op jit(solution)/shard_map/psum | solution.py:95
  290.0 0.6 dynamic-slice_bitcast_fusion
  290.6 167.9 %all-reduce.6.cloned.1.call-done = f32[256,768]{1,0:T(8,128)} async-done(((f32[256,768]{1,0:T(8,128)}), f32[256,768]{1,0:T(8,128)}) %all-reduce.6.cloned.1.call-update) | async-done | bytes 786448 | tf_op jit(solution)/shard_map/psum | solution.py:105
  458.5 1.1 multiply_reduce_fusion.2
  459.6 1.7 fusion.218
  461.3 0.0 copy-done.2
  461.3 0.5 multiply_reduce_fusion
  461.8 0.1 broadcast_subtract_fusion
  461.8 0.0 copy-done.4
  461.8 7.7 %fusion.102 = (f32[1536]{0:T(1024)S(1)}, f32[1536]{0:T(1024)S(1)}, f32[1536]{0:T(1024)S(1)}, f32[1536]{0:T(1024)S(1)}, f32[1536]{0:T(1024)S(1)}, /*index=5*/f32[...) fusion(bf16[8,7,7,1536]{3,0,2,1:T(8,128)(2,1)S(1)} %bitcast.15,, ...), kind=kLoop, calls=%fused_computation.304 | loop fusion | flops 35496960 | bytes 6185568 | tf_op jit(solution)/shard_map/reduce_sum | solution.py:60
  469.6 0.0 copy-start.5
  469.6 2.3 fusion.43
  472.0 3.5 fusion.84
  476.2 4.8 stack.199
  480.9 0.0 all-reduce.8.cloned.1.call-update
  481.0 38.0 %fusion.209 = bf16[1,8,7,7,1536]{4,1,3,2,0:T(8,128)(2,1)} fusion(f32[1536]{0:T(1024)S(1)} %get-tuple-element.60, f32[8,7,7,1536]{3,0,2,1:T(8,128)} %copy-done.5, f32[1536]{0:T(1024)S(1)} %get-tuple-element.79, f32[1536]{0:T(1024)S(1)} %get-tuple-element.98, f32[1536]{0:T(1024)S(1)} %get-tuple-element.106, f32[1536]{0:T(1024)S(1)} %get-tuple-element.105, ...), kind=kLoop, calls=%fused_computation.414 | loop fusion | flops 59609088 | bytes 3962880 | tf_op jit(solution)/shard_map/broadcast_in_dim | solution.py:113
  519.0 211.9 %all-reduce.8.cloned.1.call-done = f32[1536,49]{0,1:T(8,128)} async-done(((f32[1536,49]{0,1:T(8,128)}), f32[1536,49]{0,1:T(8,128)}) %all-reduce.8.cloned.1.call-update) | async-done | bytes 301072
  730.9 0.9 constant_dynamic-slice_fusion
  731.7 0.7 copy.9
  (62 shorter events, 0.4 us)
Async XLA Ops:
  7.2 37.8 %copy-start = (bf16[1536,768]{1,0:T(8,128)(2,1)S(1)}, bf16[1536,768]{1,0:T(8,128)(2,1)}, u32[]{:S(2)}) copy-start(bf16[1536,768]{1,0:T(8,128)(2,1)} %param.8) | copy-start | bytes 7077892
  7.2 451.3 %all-reduce.6.cloned.1.call-start = ((), (), s32[]{:S(2)}) async-start(), calls=%async_computation | async-start | bytes 1572864 | tf_op jit(solution)/shard_map/psum | solution.py:105
  11.6 32.3 %copy-start.3 = (bf16[1,8,7,7,1536]{4,1,3,2,0:T(8,128)(2,1)S(1)}, bf16[1,8,7,7,1536]{4,1,3,2,0:T(8,128)(2,1)}, u32[]{:S(2)}) copy-start(bf16[1,8,7,7,1536]{4,1,3,2,0:T(8,128)(2,1)} %param.5) | copy-start | bytes 3612676
  43.5 1.5 copy-start.1
  43.9 41.3 %copy-start.6 = (bf16[4096,768]{1,0:T(8,128)(2,1)S(1)}, bf16[4096,768]{1,0:T(8,128)(2,1)}, u32[]{:S(2)}) copy-start(bf16[4096,768]{1,0:T(8,128)(2,1)} %param.9) | copy-start | bytes 18874372
  90.4 97.4 %copy-start.7 = (s32[1,256]{1,0:T(1,128)S(1)}, s32[1,256]{1,0:T(1,128)}, u32[]{:S(2)}) copy-start(s32[1,256]{1,0:T(1,128)} %param.6) | copy-start | bytes 3076
  230.0 500.8 %all-reduce.8.cloned.1.call-start = ((), (), s32[]{:S(2)}) async-start(), calls=%async_computation.1 | async-start | bytes 688128
  458.5 2.8 copy-start.2
  459.6 2.3 copy-start.4
  469.6 2.4 copy-start.5
Sparse Core Ops, SparseCore 0:
  230.1 228.3 all-reduce.5
  481.1 249.7 all-reduce.7
where the time goes:
time: 740 us; the launch traced here: 739 us
  waiting for transfers between devices  380 us (51%)
  blocking collectives  224 us (30%)
  other arithmetic  98.7 us (13%)
  between operations  14.6 us (2%)
  matrix products  14.1 us (2%)
  local copies, waits for them, and re-layouts  7.81 us (1%)
    unnamed x3, waiting for transfers between devices  212 us
    psum x1, waiting for transfers between devices, shards(): summed = lax.psum(incomplete_gradient, 'loop')  168 us
    psum x2, blocking collectives, shards(): row_sum, target_logit = lax.psum((row_part, target_part), 'loop')  120 us
    all_gather x1, blocking collectives, shards(): lax.all_gather(query, 'loop', axis=0, tiled=True)  39.6 us
    broadcast_in_dim x1, other arithmetic, shards(): return (own_loss[None], input_grad.astype(jnp.bfloat16)[None], kernel_share)  38 us
    psum x1, blocking collectives, shards(): col_log = jnp.log(lax.psum(col_part, 'group'))  34.7 us
    reduce_sum x1, other arithmetic, forward(): centre = hidden - jnp.mean(hidden, -1, keepdims=True)  31.9 us
    psum x1, blocking collectives, shards(): col_grad = lax.psum(jnp.sum(grad, 0), 'group')  30.1 us
  transfers between devices with their start and end apart: 2, of which 2 were waited for; matrix products, arithmetic and copies ran while one was open for 5% of the time, Pallas kernels for 0%

commit v1 on v0

--- a/solution.py
+++ b/solution.py
@@ -77,8 +77,14 @@
     padded, normed, scale_inv, embedded, inv_norm = forward(pixels, kernel, projection)
     query = (embedded * inv_norm).astype(jnp.bfloat16)
     normalized_caption_vectors = normalize(captions)
+    _render_limits = lambda w_in: jnp.concatenate(
+        jax.lax.all_to_all(
+            jnp.stack([w_in for _ in range(jax.lax.axis_size("loop"))]), "loop", 0, 0
+        ),
+        0,
+    )
     similarity_scores = logit_sharpness * lax.dot_general(
-        lax.all_gather(query, "loop", axis=0, tiled=True),
+        _render_limits(query),
         normalized_caption_vectors,
         (((1,), (1,)), ((), ())),
         preferred_element_type=jnp.float32,

time: 740 us -> 729 us (0.985)
  blocking collectives: 224 us -> 186 us
  starting transfers between devices: 0.08 us -> 11.1 us
  waiting for transfers between devices: 380 us -> 389 us
    all_gather x1 -> x0, blocking collectives: 39.6 us -> none  [shards(): lax.all_gather(query, 'loop', axis=0, tiled=True)]
    all_to_all x0 -> x1, starting transfers between devices: none -> 11 us  [shards(): jax.lax.all_to_all(jnp.stack([w_in for _ in range(jax.lax.axis_size('loop...]
    all_to_all x0 -> x1, waiting for transfers between devices: none -> 9.55 us  [shards(): jax.lax.all_to_all(jnp.stack([w_in for _ in range(jax.lax.axis_size('loop...]
  transfers between devices with their start and end apart: 2 -> 3, of which waited for: 2 -> 3; matrix products, arithmetic and copies ran while one was open for 5% -> 6% of each run, Pallas kernels for 0% -> 0%
where the time goes in v1:
time: 729 us; the launch traced here: 728 us
  waiting for transfers between devices  389 us (53%)
  blocking collectives  186 us (26%)
  other arithmetic  102 us (14%)
  matrix products  17.1 us (2%)
  between operations  14.6 us (2%)
  starting transfers between devices  11.1 us (2%)
  local copies, waits for them, and re-layouts  8.6 us (1%)
    unnamed x3, waiting for transfers between devices  212 us
    psum x1, waiting for transfers between devices, shards(): summed = lax.psum(incomplete_gradient, 'loop')  168 us
    psum x2, blocking collectives, shards(): row_sum, target_logit = lax.psum((row_part, target_part), 'loop')  121 us
    broadcast_in_dim x1, other arithmetic, shards(): return (own_loss[None], input_grad.astype(jnp.bfloat16)[None], kernel_share)  38.3 us
    psum x1, blocking collectives, shards(): col_log = jnp.log(lax.psum(col_part, 'group'))  34.8 us
    reduce_sum x1, other arithmetic, forward(): centre = hidden - jnp.mean(hidden, -1, keepdims=True)  31.9 us
    psum x1, blocking collectives, shards(): col_grad = lax.psum(jnp.sum(grad, 0), 'group')  30.1 us
  transfers between devices with their start and end apart: 3, of which 3 were waited for; matrix products, arithmetic and copies ran while one was open for 6% of the time, Pallas kernels for 0%

profile of v1, /device:TPU:1, one launch (start us, length us, event | category | flops | bytes accessed | tf_op | source)
XLA Modules:
  0.0 728.1 jit_solution(10695760108254949127)
XLA Ops:
  7.2 0.0 copy-start
  7.2 1.2 convert_reduce_fusion.46
  8.4 1.5 convert_reduce_fusion.48
  9.9 1.6 convert_reduce_fusion.47
  11.5 0.0 copy-start.3
  11.5 31.9 %fusion.217 = (f32[8,7,7]{0,2,1:T(8,128)S(1)}, f32[8,7,7,1536]{3,0,2,1:T(8,128)S(1)}) fusion(f32[1536]{0:T(1024)S(1)} %get-tuple-element.107, f32[1536]{0:T(1024)S(1)} %get-tuple-element.108, f32[1536]{0:T(1024)S(1)} %get-tuple-element.61, f32[1536]{0:T(1024)S(1)} %get-tuple-element.62, f32[1536]{0:T(1024)S(1)} %get-tuple-element.63, ...), kind=kLoop, calls=%fused_computation.487 | loop fusion | flops 88510072 | bytes 3915296 | tf_op jit(solution)/shard_map/reduce_sum | solution.py:26
  43.4 0.0 copy-start.1
  43.4 0.4 multiply_reduce_fusion.1
  43.8 0.0 copy-done.3
  43.9 0.5 fusion.103
  44.3 0.6 copy-done.1
  44.9 0.0 copy-done
  44.9 0.5 multiply_reduce_fusion.3
  45.4 0.1 multiply_convert_fusion.3
  45.5 0.8 stack.185
  46.3 11.0 %all-to-all-start = ((bf16[32,8,768]{2,1,0:T(8,128)(2,1)}), bf16[32,8,768]{2,1,0:T(8,128)(2,1)S(1)}, u32[]{:S(2)}, u32[]{:S(2)}) async-start(bf16[32,8,768]{2,1,0:T(8,128)(2,1)} %stack.185), calls=%async_computation | async-start | bytes 786432 | tf_op jit(solution)/shard_map/all_to_all | solution.py:81
  57.3 0.0 all-reduce.6.cloned.1.call-start
  57.4 0.0 copy-done.6
  57.4 4.1 fusion
  61.5 9.6 %all-to-all-done = bf16[32,8,768]{2,1,0:T(8,128)(2,1)S(1)} async-done(((bf16[32,8,768]{2,1,0:T(8,128)(2,1)}), bf16[32,8,768]{2,1,0:T(8,128)(2,1)S(1)}, u32[]{:S(2)}, u32[]{:S(2)}) %all-to-all-start) | async-done | bytes 393248 | tf_op jit(solution)/shard_map/all_to_all | solution.py:81
  71.1 6.9 exponential_reduce_fusion
  77.9 34.8 %psum.35 = f32[4096]{0:T(1024)S(1)} all-reduce(f32[4096]{0:T(1024)S(1)} %get-tuple-element.114), channel_id=1, replica_groups=mesh['loop'=32,'group'=8] {'group'}, use_global_device_ids=true, to_apply=%region_6.7 | all-reduce | flops 4096 | bytes 32768 | tf_op jit(solution)/shard_map/psum | solution.py:93
  112.7 2.9 fusion.3
  115.6 61.3 %psum.36 = f32[256]{0:T(256)S(1)} all-reduce(f32[256]{0:T(256)S(1)} %fusion.3), channel_id=1, replica_groups=mesh['loop'=32,'group'=8] {'loop'}, use_global_device_ids=true, to_apply=%region_8.9 | all-reduce | flops 256 | bytes 2048 | tf_op jit(solution)/shard_map/psum | solution.py:101
  176.9 4.2 fusion.2
  181.1 30.1 %psum.38 = f32[4096]{0:T(1024)S(1)} all-reduce(f32[4096]{0:T(1024)S(1)} %get-tuple-element.9), channel_id=1, replica_groups=mesh['loop'=32,'group'=8] {'group'}, use_global_device_ids=true, to_apply=%region_12.13 | all-reduce | flops 4096 | bytes 32768 | tf_op jit(solution)/shard_map/psum | solution.py:106
  211.2 8.0 %fusion.206 = f32[256,768]{1,0:T(8,128)} fusion(bf16[4096,768]{1,0:T(8,128)(2,1)} %param.9, f32[4096]{0:T(1024)S(1)} %add_rsqrt_fusion.1, f32[256,4096]{1,0:T(8,128)} %get-tuple-element.115, f32[4096]{0:T(1024)S(1)} %psum.38, f32[256]{0:T(256)S(1)} %psum.36, s32[256]{0:T(256)S(1)} %bitcast.24, f32[4096]{0:T(1024)S(1)} %log.6), kind=kOutput, calls=%fused_computation.413 | convolution fusion | flops 1628635136 | bytes 11323392 | tf_op jit(solution)/shard_map/dot_general | solution.py:108
  219.2 0.0 all-reduce.6.cloned.1.call-update
  219.2 0.0 all-reduce.8.cloned.1.call-start
  219.3 59.7 %psum.37 = f32[256]{0:T(256)S(1)} all-reduce(f32[256]{0:T(256)S(1)} %get-tuple-element.10), channel_id=1, replica_groups=mesh['loop'=32,'group'=8] {'loop'}, use_global_device_ids=true, to_apply=%region_10.11 | all-reduce | flops 256 | bytes 2048 | tf_op jit(solution)/shard_map/psum | solution.py:101
  279.1 0.6 dynamic-slice_bitcast_fusion
  279.6 167.8 %all-reduce.6.cloned.1.call-done = f32[256,768]{1,0:T(8,128)} async-done(((f32[256,768]{1,0:T(8,128)}), f32[256,768]{1,0:T(8,128)}) %all-reduce.6.cloned.1.call-update) | async-done | bytes 786448 | tf_op jit(solution)/shard_map/psum | solution.py:111
  447.4 1.1 multiply_reduce_fusion.2
  448.5 1.7 fusion.219
  450.2 0.0 copy-done.2
  450.2 0.5 multiply_reduce_fusion
  450.7 0.1 broadcast_subtract_fusion
  450.8 0.0 copy-done.4
  450.8 7.7 %fusion.102 = (f32[1536]{0:T(1024)S(1)}, f32[1536]{0:T(1024)S(1)}, f32[1536]{0:T(1024)S(1)}, f32[1536]{0:T(1024)S(1)}, f32[1536]{0:T(1024)S(1)}, /*index=5*/f32[...) fusion(bf16[8,7,7,1536]{3,0,2,1:T(8,128)(2,1)S(1)} %bitcast.19,, ...), kind=kLoop, calls=%fused_computation.304 | loop fusion | flops 35496960 | bytes 6185568 | tf_op jit(solution)/shard_map/reduce_sum | solution.py:60
  458.5 0.0 copy-start.5
  458.5 2.3 fusion.43
  460.8 3.5 fusion.84
  465.0 4.8 stack.235
  469.8 0.0 all-reduce.8.cloned.1.call-update
  469.8 38.3 %fusion.209 = bf16[1,8,7,7,1536]{4,1,3,2,0:T(8,128)(2,1)} fusion(f32[1536]{0:T(1024)S(1)} %get-tuple-element.60, f32[8,7,7,1536]{3,0,2,1:T(8,128)} %copy-done.5, f32[1536]{0:T(1024)S(1)} %get-tuple-element.79, f32[1536]{0:T(1024)S(1)} %get-tuple-element.98, f32[1536]{0:T(1024)S(1)} %get-tuple-element.106, f32[1536]{0:T(1024)S(1)} %get-tuple-element.105, ...), kind=kLoop, calls=%fused_computation.414 | loop fusion | flops 59609088 | bytes 3962880 | tf_op jit(solution)/shard_map/broadcast_in_dim | solution.py:119
  508.1 211.6 %all-reduce.8.cloned.1.call-done = f32[1536,49]{0,1:T(8,128)} async-done(((f32[1536,49]{0,1:T(8,128)}), f32[1536,49]{0,1:T(8,128)}) %all-reduce.8.cloned.1.call-update) | async-done | bytes 301072
  719.7 0.9 constant_dynamic-slice_fusion
  720.6 0.7 copy.9
  (62 shorter events, 0.4 us)
Async XLA Ops:
  7.2 37.7 %copy-start = (bf16[1536,768]{1,0:T(8,128)(2,1)S(1)}, bf16[1536,768]{1,0:T(8,128)(2,1)}, u32[]{:S(2)}) copy-start(bf16[1536,768]{1,0:T(8,128)(2,1)} %param.8) | copy-start | bytes 7077892
  11.5 32.3 %copy-start.3 = (bf16[1,8,7,7,1536]{4,1,3,2,0:T(8,128)(2,1)S(1)}, bf16[1,8,7,7,1536]{4,1,3,2,0:T(8,128)(2,1)}, u32[]{:S(2)}) copy-start(bf16[1,8,7,7,1536]{4,1,3,2,0:T(8,128)(2,1)} %param.5) | copy-start | bytes 3612676
  43.4 1.5 copy-start.1
  44.9 12.5 %copy-start.6 = (s32[1,256]{1,0:T(1,128)S(1)}, s32[1,256]{1,0:T(1,128)}, u32[]{:S(2)}) copy-start(s32[1,256]{1,0:T(1,128)} %param.6) | copy-start | bytes 3076
  46.3 24.8 %all-to-all-start = ((bf16[32,8,768]{2,1,0:T(8,128)(2,1)}), bf16[32,8,768]{2,1,0:T(8,128)(2,1)S(1)}, u32[]{:S(2)}, u32[]{:S(2)}) async-start(bf16[32,8,768]{2,1,0:T(8,128)(2,1)} %stack.185), calls=%async_computation | async-start | bytes 786432 | tf_op jit(solution)/shard_map/all_to_all | solution.py:81
  57.3 390.1 %all-reduce.6.cloned.1.call-start = ((), (), s32[]{:S(2)}) async-start(), calls=%async_computation.1 | async-start | bytes 1572864 | tf_op jit(solution)/shard_map/psum | solution.py:111
  219.2 500.5 %all-reduce.8.cloned.1.call-start = ((), (), s32[]{:S(2)}) async-start(), calls=%async_computation.2 | async-start | bytes 688128
  447.4 2.8 copy-start.2
  448.5 2.3 copy-start.4
  458.5 2.4 copy-start.5
Sparse Core Ops, SparseCore 0:
  219.4 228.0 all-reduce.5
  469.9 249.7 all-reduce.7
